TPU v7x, 256 devices: a whole 4x4x8 slice. The times are simulated.
256 devices in a mesh: expert: 64 (over x, z, core), hidden: 4 (over y).
Axes of the slice: x: 4, y: 4, z: 8, core: 2. Of those that a mesh axis runs over, the one named last changes fastest.
Arguments:
- tokens: bfloat16 [1024, 7168], P('expert', 'hidden'), may hold values from -6 to 6
- routes: int32 [1024, 8], P('expert'), may hold values from 0 to 63, as said below
- combine: float32 [1024, 8], P('expert'), may hold values from 0.05 to 0.5
- w_gate: bfloat16 [64, 7168, 1024], P('expert', None, 'hidden'), may hold values from -0.0625 to 0.0625
- w_up: bfloat16 [64, 7168, 1024], P('expert', None, 'hidden'), may hold values from -0.0625 to 0.0625
- w_down: bfloat16 [64, 1024, 7168], P('expert', 'hidden'), may hold values from -0.1875 to 0.1875
- cotangent: bfloat16 [1024, 7168], P('expert', 'hidden'), may hold values from -6 to 6
Outputs:
- output: bfloat16 [1024, 7168], P('expert', 'hidden')
- grad_tokens: bfloat16 [1024, 7168], P('expert', 'hidden')
Inputs may be any that keep to these rules, and one draw needn't show every extreme that they name: `routes`: each row names 8 different experts. In each aligned block of 16 rows (the rows of one device) no expert is named by more than 4 rows, and the same expert is named by exactly 4 rows in every block.
All inputs are finite; a program needn't handle non-finite values.
Results may differ from a plain program's by a relative error of at most 0.012.
Values may be sent and summed in bfloat16 or wider, within the bound.
No kernel may reach another device: no remote copies, remote signals or barrier semaphores. Data moves between devices by JAX's collectives and lax.ppermute only.
A program may use at most 128 MiB of HBM per device.

v0:
```python
import jax
import jax.numpy as jnp
from jax import lax
from jax.sharding import PartitionSpec as P


def per_device(tokens, routes, combine, w_gate, w_up, w_down, cotangent):
    tok_rows = tokens.shape[0]
    top_count = routes.shape[1]
    local_experts = w_gate.shape[0]
    sources = lax.axis_size("expert")
    experts = local_experts * sources
    pair_count = tok_rows * top_count
    capacity = 2 * pair_count // experts
    flat_routes = routes.reshape(pair_count)
    onehot = (flat_routes[:, None] == jnp.arange(experts, dtype=jnp.int32)[None, :]).astype(
        jnp.int32
    )
    slot_rank = jnp.sum((jnp.cumsum(onehot, axis=0) - 1) * onehot, axis=1)
    target = flat_routes * capacity + slot_rank
    slot_table = (
        jnp.full((experts * capacity,), pair_count, jnp.int32)
        .at[target]
        .set(jnp.arange(pair_count, dtype=jnp.int32))
    )
    source_rows = slot_table // top_count

    def pack_rows(values):
        padded = jnp.concatenate([values, jnp.zeros((1, values.shape[1]), values.dtype)], axis=0)
        return padded[source_rows].reshape(experts, capacity, values.shape[1])

    def to_local(arrived):
        columns = arrived.shape[2]
        sectioned = arrived.reshape(sources, local_experts, capacity, columns).transpose(1, 0, 2, 3)
        return sectioned.reshape(local_experts, sources * capacity, columns)

    def to_global(leaving):
        columns = leaving.shape[2]
        sectioned = leaving.reshape(local_experts, sources, capacity, columns).transpose(1, 0, 2, 3)
        return sectioned.reshape(experts, capacity, columns)

    def unpack(returned):
        flattened = returned.reshape(experts * capacity, returned.shape[2])
        picked = (
            flattened[target].astype(jnp.float32).reshape(tok_rows, top_count, returned.shape[2])
        )
        return jnp.sum(picked * combine[:, :, None], axis=1).astype(jnp.bfloat16)

    full_tokens, full_grads = (
        lax.all_gather(tokens, "hidden", axis=1, tiled=True),
        lax.all_gather(cotangent, "hidden", axis=1, tiled=True),
    )
    arrived_x, arrived_dy = (
        lax.all_to_all(pack_rows(full_tokens), "expert", split_axis=0, concat_axis=0, tiled=True),
        lax.all_to_all(pack_rows(full_grads), "expert", split_axis=0, concat_axis=0, tiled=True),
    )
    arrived_x = to_local(arrived_x)
    arrived_dy = to_local(arrived_dy)
    gate_pre = jnp.einsum("erd,edf->erf", arrived_x, w_gate, preferred_element_type=jnp.float32)
    up_pre = jnp.einsum("erd,edf->erf", arrived_x, w_up, preferred_element_type=jnp.float32)
    back_hidden = jnp.einsum("erd,efd->erf", arrived_dy, w_down, preferred_element_type=jnp.float32)
    sigmoid_gate = jax.nn.sigmoid(gate_pre)
    activated = gate_pre * sigmoid_gate
    hidden_act = (activated * up_pre).astype(jnp.bfloat16)
    out_terms = jnp.einsum(
        "erf,efd->erd", hidden_act, w_down, preferred_element_type=jnp.float32
    ).astype(jnp.bfloat16)
    grad_gate = (
        back_hidden * up_pre * sigmoid_gate * (1.0 + gate_pre * (1.0 - sigmoid_gate))
    ).astype(jnp.bfloat16)
    grad_up = (back_hidden * activated).astype(jnp.bfloat16)
    out_share = (
        lax.psum_scatter(out_terms, "hidden", scatter_dimension=2, tiled=True)
        .astype(jnp.float32)
        .astype(jnp.bfloat16)
    )
    out_back = lax.all_to_all(
        to_global(out_share), "expert", split_axis=0, concat_axis=0, tiled=True
    )
    grad_terms = jnp.einsum("erf,edf->erd", grad_gate, w_gate, preferred_element_type=jnp.float32)
    grad_terms = grad_terms + jnp.einsum(
        "erf,edf->erd", grad_up, w_up, preferred_element_type=jnp.float32
    )
    grad_share = lax.psum_scatter(
        grad_terms.astype(jnp.bfloat16), "hidden", scatter_dimension=2, tiled=True
    )
    grad_back = lax.all_to_all(
        to_global(grad_share), "expert", split_axis=0, concat_axis=0, tiled=True
    )
    return (unpack(out_back), unpack(grad_back))


def solution(mesh):
    return jax.shard_map(
        per_device,
        mesh=mesh,
        in_specs=(
            P("expert", "hidden"),
            P("expert", None),
            P("expert", None),
            P("expert", None, "hidden"),
            P("expert", None, "hidden"),
            P("expert", "hidden", None),
            P("expert", "hidden"),
        ),
        out_specs=(P("expert", "hidden"), P("expert", "hidden")),
        check_vma=False,
    )
```

profile of v0, /device:TPU:1, one launch (start us, length us, event | category | flops | bytes accessed | tf_op | source)
XLA Modules:
  0.0 376.7 jit_solution(7384329820560106243)
XLA Ops:
  7.2 0.8 copy.13
  9.3 1.0 scatter_custom_fusion
  10.3 11.0 %all_gather.6 = bf16[16,7168]{1,0:T(8,128)(2,1)S(1)} all-gather(bf16[16,1792]{1,0:T(8,128)(2,1)} %param.7), channel_id=1, replica_groups=mesh['expert'=64,'hidden'=4] {'hidden'}, dimensions={1}, use_global_device_ids=true | all-gather | bytes 286720 | tf_op jit(solution)/shard_map/all_gather | solution.py:50
  21.4 4.7 %gather_fusion = bf16[256,7168]{1,0:T(8,128)(2,1)} fusion(bf16[17,7168]{1,0:T(8,128)(2,1)S(1)} %concatenate.6, s32[1024]{0:T(1024)S(1)} %pad_clamp_fusion.1), kind=kCustom, calls=%fused_computation | custom fusion | bytes 7341056 | tf_op jit(solution)/shard_map/gather | solution.py:30
  26.1 7.0 %reshape.108 = bf16[64,4,7168]{2,1,0:T(4,128)(2,1)} reshape(bf16[256,7168]{1,0:T(8,128)(2,1)} %gather_fusion) | data formatting | bytes 7340032 | tf_op jit(solution)/shard_map/reshape | solution.py:30
  33.1 15.2 %all-to-all-start = ((bf16[64,4,7168]{2,1,0:T(4,128)(2,1)}), bf16[64,4,7168]{2,1,0:T(4,128)(2,1)}, u32[]{:S(2)}, u32[]{:S(2)}) async-start(bf16[64,4,7168]{2,1,0:T(4,128)(2,1)} %reshape.108), calls=%async_computation | async-start | bytes 7340032 | tf_op jit(solution)/shard_map/all_to_all | solution.py:54
  48.2 10.5 %all_gather.7 = bf16[16,7168]{1,0:T(8,128)(2,1)S(1)} all-gather(bf16[16,1792]{1,0:T(8,128)(2,1)S(1)} %copy-done.4), channel_id=1, replica_groups=mesh['expert'=64,'hidden'=4] {'hidden'}, dimensions={1}, use_global_device_ids=true | all-gather | bytes 286720 | tf_op jit(solution)/shard_map/all_gather | solution.py:51
  58.8 4.8 %gather_fusion.2 = bf16[256,7168]{1,0:T(8,128)(2,1)} fusion(bf16[17,7168]{1,0:T(8,128)(2,1)S(1)} %concatenate.7, s32[1024]{0:T(1024)S(1)} %pad_clamp_fusion.1), kind=kCustom, calls=%fused_computation.2 | custom fusion | bytes 7341056 | tf_op jit(solution)/shard_map/gather | solution.py:30
  63.6 7.0 %reshape.114 = bf16[64,4,7168]{2,1,0:T(4,128)(2,1)} reshape(bf16[256,7168]{1,0:T(8,128)(2,1)} %gather_fusion.2) | data formatting | bytes 7340032 | tf_op jit(solution)/shard_map/reshape | solution.py:30
  70.6 62.3 %all-to-all-done = bf16[64,4,7168]{2,1,0:T(4,128)(2,1)} async-done(((bf16[64,4,7168]{2,1,0:T(4,128)(2,1)}), bf16[64,4,7168]{2,1,0:T(4,128)(2,1)}, u32[]{:S(2)}, u32[]{:S(2)}) %all-to-all-start) | async-done | bytes 3670048 | tf_op jit(solution)/shard_map/all_to_all | solution.py:54
  132.9 5.9 %all-to-all-start.2 = ((bf16[64,4,7168]{2,1,0:T(4,128)(2,1)}), bf16[64,4,7168]{2,1,0:T(4,128)(2,1)}, u32[]{:S(2)}, u32[]{:S(2)}) async-start(bf16[64,4,7168]{2,1,0:T(4,128)(2,1)} %reshape.114), calls=%async_computation.3 | async-start | bytes 7340032 | tf_op jit(solution)/shard_map/all_to_all | solution.py:55
  139.0 6.7 %reshape.109 = bf16[256,7168]{1,0:T(8,128)(2,1)} reshape(bf16[64,4,7168]{2,1,0:T(4,128)(2,1)} %all-to-all-done) | data formatting | bytes 7340032 | tf_op jit(solution)/shard_map/reshape
  145.8 4.4 %fusion.11 = f32[256,256]{1,0:T(8,128)S(1)} fusion(bf16[256,7168]{1,0:T(8,128)(2,1)} %reshape.109, bf16[1,7168,256]{2,1,0:T(8,128)(2,1)} %param.10), kind=kOutput, calls=%fused_computation.18 | convolution fusion | flops 939524096 | bytes 7602176 | tf_op jit(solution)/shard_map/erd,edf->erf/dot_general | solution.py:59
  150.2 0.9 copy-done.2
  151.1 1.1 fusion.7
  152.2 71.3 %all-to-all-done.2 = bf16[64,4,7168]{2,1,0:T(4,128)(2,1)} async-done(((bf16[64,4,7168]{2,1,0:T(4,128)(2,1)}), bf16[64,4,7168]{2,1,0:T(4,128)(2,1)}, u32[]{:S(2)}, u32[]{:S(2)}) %all-to-all-start.2) | async-done | bytes 3670048 | tf_op jit(solution)/shard_map/all_to_all | solution.py:55
  223.4 6.7 %reshape.115 = bf16[256,7168]{1,0:T(8,128)(2,1)} reshape(bf16[64,4,7168]{2,1,0:T(4,128)(2,1)} %all-to-all-done.2) | data formatting | bytes 7340032 | tf_op jit(solution)/shard_map/reshape.19
  230.2 4.4 %fusion.3 = f32[256,256]{1,0:T(8,128)S(1)} fusion(bf16[256,7168]{1,0:T(8,128)(2,1)} %reshape.115, bf16[1,256,7168]{2,1,0:T(8,128)(2,1)} %param.12), kind=kOutput, calls=%fused_computation.10 | convolution fusion | flops 939524096 | bytes 7602176 | tf_op jit(solution)/shard_map/erd,efd->erf/dot_general | solution.py:61
  234.6 1.2 fusion.9
  235.8 0.9 copy-done.3
  236.7 3.0 fusion.2
  239.7 5.0 %fusion.1 = bf16[1,256,7168]{2,1,0:T(8,128)(2,1)} fusion(bf16[1,256,7168]{2,1,0:T(8,128)(2,1)} %param.12, f32[256,256]{1,0:T(8,128)S(1)} %fusion.7, f32[256,256]{1,0:T(8,128)S(1)} %fusion.11), kind=kOutput, calls=%fused_computation.8 | convolution fusion | flops 941752320 | bytes 7864320 | tf_op jit(solution)/shard_map/erf,efd->erd/dot_general | solution.py:65
  244.7 36.1 %reduce-scatter.5.cloned.1.call-done = bf16[1,256,1792]{2,1,0:T(8,128)(2,1)} async-done(((bf16[1,256,7168]{2,1,0:T(8,128)(2,1)}), bf16[1,256,1792]{2,1,0:T(8,128)(2,1)}) %reduce-scatter.5.cloned.1.call-update) | async-done | bytes 917520 | tf_op jit(solution)/shard_map/reduce_scatter | solution.py:84
  280.8 2.5 reshape_transpose_reshape.9
  283.3 10.7 %all-to-all-start.3 = ((bf16[64,4,1792]{2,1,0:T(4,128)(2,1)}), bf16[64,4,1792]{2,1,0:T(4,128)(2,1)S(1)}, u32[]{:S(2)}, u32[]{:S(2)}) async-start(bf16[64,4,1792]{2,1,0:T(4,128)(2,1)} %reshape_transpose_reshape.9), calls=%async_computation.5 | async-start | bytes 1835008 | tf_op jit(solution)/shard_map/all_to_all | solution.py:87
  294.1 34.2 %reduce-scatter.3.cloned.1.call-done = bf16[1,256,1792]{2,1,0:T(8,128)(2,1)} async-done(((bf16[1,256,7168]{2,1,0:T(8,128)(2,1)}), bf16[1,256,1792]{2,1,0:T(8,128)(2,1)}) %reduce-scatter.3.cloned.1.call-update) | async-done | bytes 917520 | tf_op jit(solution)/shard_map/reduce_scatter | solution.py:73
  328.3 2.5 reshape_transpose_reshape.8
  330.8 10.7 %all-to-all-start.1 = ((bf16[64,4,1792]{2,1,0:T(4,128)(2,1)}), bf16[64,4,1792]{2,1,0:T(4,128)(2,1)S(1)}, u32[]{:S(2)}, u32[]{:S(2)}) async-start(bf16[64,4,1792]{2,1,0:T(4,128)(2,1)} %reshape_transpose_reshape.8), calls=%async_computation.2 | async-start | bytes 1835008 | tf_op jit(solution)/shard_map/all_to_all | solution.py:77
  341.9 0.9 gather_fusion.3
  342.8 24.5 %all-to-all-done.1 = bf16[64,4,1792]{2,1,0:T(4,128)(2,1)S(1)} async-done(((bf16[64,4,1792]{2,1,0:T(4,128)(2,1)}), bf16[64,4,1792]{2,1,0:T(4,128)(2,1)S(1)}, u32[]{:S(2)}, u32[]{:S(2)}) %all-to-all-start.1) | async-done | bytes 917536 | tf_op jit(solution)/shard_map/all_to_all | solution.py:77
  367.5 0.9 gather_fusion.1
  368.4 1.4 fusion.13
  (32 shorter events, 2.3 us)
Async XLA Ops:
  33.1 15.2 %copy-start.4 = (bf16[16,1792]{1,0:T(8,128)(2,1)S(1)}, bf16[16,1792]{1,0:T(8,128)(2,1)}, u32[]{:S(2)}) copy-start(bf16[16,1792]{1,0:T(8,128)(2,1)} %param.13) | copy-start | bytes 172036
  33.1 99.8 %all-to-all-start = ((bf16[64,4,7168]{2,1,0:T(4,128)(2,1)}), bf16[64,4,7168]{2,1,0:T(4,128)(2,1)}, u32[]{:S(2)}, u32[]{:S(2)}) async-start(bf16[64,4,7168]{2,1,0:T(4,128)(2,1)} %reshape.108), calls=%async_computation | async-start | bytes 7340032 | tf_op jit(solution)/shard_map/all_to_all | solution.py:54
  132.9 90.6 %all-to-all-start.2 = ((bf16[64,4,7168]{2,1,0:T(4,128)(2,1)}), bf16[64,4,7168]{2,1,0:T(4,128)(2,1)}, u32[]{:S(2)}, u32[]{:S(2)}) async-start(bf16[64,4,7168]{2,1,0:T(4,128)(2,1)} %reshape.114), calls=%async_computation.3 | async-start | bytes 7340032 | tf_op jit(solution)/shard_map/all_to_all | solution.py:55
  138.8 142.0 %reduce-scatter.5.cloned.1.call-start = ((), (), s32[]{:S(2)}) async-start(), calls=%async_computation.7 | async-start | bytes 4587520 | tf_op jit(solution)/shard_map/reduce_scatter | solution.py:84
  145.8 4.4 %copy-start = (bf16[256,7168]{1,0:T(8,128)(2,1)S(1)}, bf16[256,7168]{1,0:T(8,128)(2,1)}, u32[]{:S(2)}) copy-start(bf16[256,7168]{1,0:T(8,128)(2,1)} %reshape.109) | copy-start | bytes 11010052
  145.8 5.3 %copy-start.2 = (bf16[1,7168,256]{2,1,0:T(8,128)(2,1)S(1)}, bf16[1,7168,256]{2,1,0:T(8,128)(2,1)}, u32[]{:S(2)}) copy-start(bf16[1,7168,256]{2,1,0:T(8,128)(2,1)} %param.11) | copy-start | bytes 11010052
  230.2 4.5 %copy-start.1 = (bf16[1,7168,256]{2,1,0:T(8,128)(2,1)S(1)}, bf16[1,7168,256]{2,1,0:T(8,128)(2,1)}, u32[]{:S(2)}) copy-start(bf16[1,7168,256]{2,1,0:T(8,128)(2,1)} %param.10) | copy-start | bytes 11010052
  234.6 2.0 copy-start.3
  239.7 88.6 %reduce-scatter.3.cloned.1.call-start = ((), (), s32[]{:S(2)}) async-start(), calls=%async_computation.6 | async-start | bytes 4587520 | tf_op jit(solution)/shard_map/reduce_scatter | solution.py:73
  244.7 96.8 %copy-start.5 = (f32[16,8]{0,1:T(8,128)S(1)}, f32[16,8]{0,1:T(8,128)}, u32[]{:S(2)}) copy-start(f32[16,8]{0,1:T(8,128)} %param.9) | copy-start | bytes 1540
  283.3 47.5 %all-to-all-start.3 = ((bf16[64,4,1792]{2,1,0:T(4,128)(2,1)}), bf16[64,4,1792]{2,1,0:T(4,128)(2,1)S(1)}, u32[]{:S(2)}, u32[]{:S(2)}) async-start(bf16[64,4,1792]{2,1,0:T(4,128)(2,1)} %reshape_transpose_reshape.9), calls=%async_computation.5 | async-start | bytes 1835008 | tf_op jit(solution)/shard_map/all_to_all | solution.py:87
  330.8 36.5 %all-to-all-start.1 = ((bf16[64,4,1792]{2,1,0:T(4,128)(2,1)}), bf16[64,4,1792]{2,1,0:T(4,128)(2,1)S(1)}, u32[]{:S(2)}, u32[]{:S(2)}) async-start(bf16[64,4,1792]{2,1,0:T(4,128)(2,1)} %reshape_transpose_reshape.8), calls=%async_computation.2 | async-start | bytes 1835008 | tf_op jit(solution)/shard_map/all_to_all | solution.py:77
Sparse Core Ops, SparseCore 0:
  239.8 40.9 reduce-scatter.4
  283.4 44.8 reduce-scatter.2
where the time goes:
time: 378 us; the launch traced here: 377 us
  waiting for transfers between devices  228 us (60%)
  local copies, waits for them, and re-layouts  48.1 us (13%)
  starting transfers between devices  42.8 us (11%)
  blocking collectives  21.5 us (6%)
  matrix products  19.1 us (5%)
  between operations  14.2 us (4%)
    all_to_all x1, waiting for transfers between devices, per_device(): lax.all_to_all(pack_rows(full_grads), 'expert', split_axis=0, concat_axis...  71.3 us
    all_to_all x1, waiting for transfers between devices, per_device(): lax.all_to_all(pack_rows(full_tokens), 'expert', split_axis=0, concat_axi...  62.3 us
    reduce_scatter x1, waiting for transfers between devices, per_device(): lax.psum_scatter(grad_terms.astype(jnp.bfloat16), 'hidden', scatter_dimen...  36.1 us
    reduce_scatter x1, waiting for transfers between devices, per_device(): lax.psum_scatter(out_terms, 'hidden', scatter_dimension=2, tiled=True)  34.2 us
    all_to_all x1, waiting for transfers between devices, per_device(): lax.all_to_all(to_global(out_share), 'expert', split_axis=0, concat_axis=...  24.5 us
    all_to_all x1, starting transfers between devices, per_device(): lax.all_to_all(pack_rows(full_tokens), 'expert', split_axis=0, concat_axi...  15.2 us
    reshape x2, local copies, waits for them, and re-layouts, pack_rows(): return padded[source_rows].reshape(experts, capacity, values.shape[1])  14 us
    all_gather x1, blocking collectives, per_device(): lax.all_gather(tokens, 'hidden', axis=1, tiled=True)  11 us
  transfers between devices with their start and end apart: 6, of which 5 were waited for; matrix products, arithmetic and copies ran while one was open for 9% of the time, Pallas kernels for 0%

commit v1 on v0

--- a/solution.py
+++ b/solution.py
@@ -48,7 +48,9 @@
 
     full_tokens, full_grads = (
         lax.all_gather(tokens, "hidden", axis=1, tiled=True),
-        lax.all_gather(cotangent, "hidden", axis=1, tiled=True),
+        jnp.concatenate(
+            lax.all_to_all(jnp.stack([cotangent] * lax.axis_size("hidden")), "hidden", 0, 0), axis=1
+        ),
     )
     arrived_x, arrived_dy = (
         lax.all_to_all(pack_rows(full_tokens), "expert", split_axis=0, concat_axis=0, tiled=True),

time: 378 us -> 337 us (0.89)
  waiting for transfers between devices: 228 us -> 198 us
  blocking collectives: 21.5 us -> 10.1 us
    reduce_scatter x1, waiting for transfers between devices: 34.2 us -> 0.02 us  [per_device(): lax.psum_scatter(out_terms, 'hidden', scatter_dimension=2, tiled=True)]
    all_to_all x1, waiting for transfers between devices: 24.5 us -> 0.01 us  [per_device(): lax.all_to_all(to_global(out_share), 'expert', split_axis=0, concat_axis=...]
    all_to_all x1, waiting for transfers between devices: 0.01 us -> 24.5 us  [per_device(): lax.all_to_all(to_global(grad_share), 'expert', split_axis=0, concat_axis...]
    all_to_all x1, waiting for transfers between devices: 62.3 us -> 72.8 us  [per_device(): lax.all_to_all(pack_rows(full_tokens), 'expert', split_axis=0, concat_axi...]
    all_gather x1 -> x0, blocking collectives: 10.5 us -> none  [per_device(): lax.all_gather(cotangent, 'hidden', axis=1, tiled=True)]
    all_to_all x0 -> x1, starting transfers between devices: none -> 5 us  [per_device(): lax.all_to_all(jnp.stack([cotangent] * lax.axis_size('hidden')), 'hidden'...]
    all_to_all x1, starting transfers between devices: 10.7 us -> 5.74 us  [per_device(): lax.all_to_all(to_global(out_share), 'expert', split_axis=0, concat_axis=...]
    all_to_all x1, waiting for transfers between devices: 71.3 us -> 67.2 us  [per_device(): lax.all_to_all(pack_rows(full_grads), 'expert', split_axis=0, concat_axis...]
  transfers between devices with their start and end apart: 6 -> 7, of which waited for: 5 -> 4; matrix products, arithmetic and copies ran while one was open for 9% -> 19% of each run, Pallas kernels for 0% -> 0%
where the time goes in v1:
time: 337 us; the launch traced here: 335 us
  waiting for transfers between devices  198 us (59%)
  local copies, waits for them, and re-layouts  50.5 us (15%)
  starting transfers between devices  43.4 us (13%)
  matrix products  17.1 us (5%)
  between operations  14.2 us (4%)
  blocking collectives  10.1 us (3%)
    all_to_all x1, waiting for transfers between devices, per_device(): lax.all_to_all(pack_rows(full_tokens), 'expert', split_axis=0, concat_axi...  72.8 us
    all_to_all x1, waiting for transfers between devices, per_device(): lax.all_to_all(pack_rows(full_grads), 'expert', split_axis=0, concat_axis...  67.2 us
    reduce_scatter x1, waiting for transfers between devices, per_device(): lax.psum_scatter(grad_terms.astype(jnp.bfloat16), 'hidden', scatter_dimen...  32.9 us
    all_to_all x1, waiting for transfers between devices, per_device(): lax.all_to_all(to_global(grad_share), 'expert', split_axis=0, concat_axis...  24.5 us
    all_to_all x1, starting transfers between devices, per_device(): lax.all_to_all(pack_rows(full_tokens), 'expert', split_axis=0, concat_axi...  15.8 us
    reshape x2, local copies, waits for them, and re-layouts, pack_rows(): return padded[source_rows].reshape(experts, capacity, values.shape[1])  14 us
    all_to_all x1, starting transfers between devices, per_device(): lax.all_to_all(to_global(grad_share), 'expert', split_axis=0, concat_axis...  10.7 us
    all_gather x1, blocking collectives, per_device(): lax.all_gather(tokens, 'hidden', axis=1, tiled=True)  10.1 us
  transfers between devices with their start and end apart: 7, of which 4 were waited for; matrix products, arithmetic and copies ran while one was open for 19% of the time, Pallas kernels for 0%

profile of v1, /device:TPU:1, one launch (start us, length us, event | category | flops | bytes accessed | tf_op | source)
XLA Modules:
  0.0 335.5 jit_solution(4621534965380974733)
XLA Ops:
  7.2 1.5 stack.2
  8.7 5.0 %all-to-all-start.2 = ((bf16[4,16,1792]{2,1,0:T(8,128)(2,1)}), bf16[4,16,1792]{2,1,0:T(8,128)(2,1)S(1)}, u32[]{:S(2)}, u32[]{:S(2)}) async-start(bf16[4,16,1792]{2,1,0:T(8,128)(2,1)} %stack.2), calls=%async_computation.3 | async-start | bytes 458752 | tf_op jit(solution)/shard_map/all_to_all | solution.py:52
  15.9 1.0 scatter_custom_fusion
  16.9 10.1 %all_gather.3 = bf16[16,7168]{1,0:T(8,128)(2,1)S(1)} all-gather(bf16[16,1792]{1,0:T(8,128)(2,1)} %param.7), channel_id=1, replica_groups=mesh['expert'=64,'hidden'=4] {'hidden'}, dimensions={1}, use_global_device_ids=true | all-gather | bytes 286720 | tf_op jit(solution)/shard_map/all_gather | solution.py:50
  27.0 4.7 %gather_fusion = bf16[256,7168]{1,0:T(8,128)(2,1)} fusion(bf16[17,7168]{1,0:T(8,128)(2,1)S(1)} %concatenate.6, s32[1024]{0:T(1024)S(1)} %pad_clamp_fusion.1), kind=kCustom, calls=%fused_computation | custom fusion | bytes 7341056 | tf_op jit(solution)/shard_map/gather | solution.py:30
  31.6 7.0 %reshape.116 = bf16[64,4,7168]{2,1,0:T(4,128)(2,1)} reshape(bf16[256,7168]{1,0:T(8,128)(2,1)} %gather_fusion) | data formatting | bytes 7340032 | tf_op jit(solution)/shard_map/reshape | solution.py:30
  38.7 15.8 %all-to-all-start = ((bf16[64,4,7168]{2,1,0:T(4,128)(2,1)}), bf16[64,4,7168]{2,1,0:T(4,128)(2,1)}, u32[]{:S(2)}, u32[]{:S(2)}) async-start(bf16[64,4,7168]{2,1,0:T(4,128)(2,1)} %reshape.116), calls=%async_computation | async-start | bytes 7340032 | tf_op jit(solution)/shard_map/all_to_all | solution.py:56
  54.5 4.8 %gather_fusion.2 = bf16[256,7168]{1,0:T(8,128)(2,1)} fusion(bf16[17,7168]{1,0:T(8,128)(2,1)S(1)} %concatenate.7, s32[1024]{0:T(1024)S(1)} %pad_clamp_fusion.1), kind=kCustom, calls=%fused_computation.2 | custom fusion | bytes 7341056 | tf_op jit(solution)/shard_map/gather | solution.py:30
  59.2 7.0 %reshape.124 = bf16[64,4,7168]{2,1,0:T(4,128)(2,1)} reshape(bf16[256,7168]{1,0:T(8,128)(2,1)} %gather_fusion.2) | data formatting | bytes 7340032 | tf_op jit(solution)/shard_map/reshape | solution.py:30
  66.2 72.8 %all-to-all-done = bf16[64,4,7168]{2,1,0:T(4,128)(2,1)} async-done(((bf16[64,4,7168]{2,1,0:T(4,128)(2,1)}), bf16[64,4,7168]{2,1,0:T(4,128)(2,1)}, u32[]{:S(2)}, u32[]{:S(2)}) %all-to-all-start) | async-done | bytes 3670048 | tf_op jit(solution)/shard_map/all_to_all | solution.py:56
  139.1 5.9 %all-to-all-start.3 = ((bf16[64,4,7168]{2,1,0:T(4,128)(2,1)}), bf16[64,4,7168]{2,1,0:T(4,128)(2,1)}, u32[]{:S(2)}, u32[]{:S(2)}) async-start(bf16[64,4,7168]{2,1,0:T(4,128)(2,1)} %reshape.124), calls=%async_computation.4 | async-start | bytes 7340032 | tf_op jit(solution)/shard_map/all_to_all | solution.py:57
  145.2 6.7 %reshape.117 = bf16[256,7168]{1,0:T(8,128)(2,1)} reshape(bf16[64,4,7168]{2,1,0:T(4,128)(2,1)} %all-to-all-done) | data formatting | bytes 7340032 | tf_op jit(solution)/shard_map/reshape
  151.9 4.4 %fusion.11 = f32[256,256]{1,0:T(8,128)S(1)} fusion(bf16[256,7168]{1,0:T(8,128)(2,1)} %reshape.117, bf16[1,7168,256]{2,1,0:T(8,128)(2,1)} %param.10), kind=kOutput, calls=%fused_computation.18 | convolution fusion | flops 939524096 | bytes 7602176 | tf_op jit(solution)/shard_map/erd,edf->erf/dot_general | solution.py:61
  156.4 0.9 copy-done.3
  157.2 1.1 fusion.7
  158.4 0.9 copy-done.1
  159.3 3.0 fusion.1
  162.4 67.2 %all-to-all-done.3 = bf16[64,4,7168]{2,1,0:T(4,128)(2,1)} async-done(((bf16[64,4,7168]{2,1,0:T(4,128)(2,1)}), bf16[64,4,7168]{2,1,0:T(4,128)(2,1)}, u32[]{:S(2)}, u32[]{:S(2)}) %all-to-all-start.3) | async-done | bytes 3670048 | tf_op jit(solution)/shard_map/all_to_all | solution.py:57
  229.6 6.7 %reshape.125 = bf16[256,7168]{1,0:T(8,128)(2,1)} reshape(bf16[64,4,7168]{2,1,0:T(4,128)(2,1)} %all-to-all-done.3) | data formatting | bytes 7340032 | tf_op jit(solution)/shard_map/reshape.22
  236.4 4.4 %fusion.3 = f32[256,256]{1,0:T(8,128)S(1)} fusion(bf16[256,7168]{1,0:T(8,128)(2,1)} %reshape.125, bf16[1,256,7168]{2,1,0:T(8,128)(2,1)} %param.12), kind=kOutput, calls=%fused_computation.10 | convolution fusion | flops 939524096 | bytes 7602176 | tf_op jit(solution)/shard_map/erd,efd->erf/dot_general | solution.py:63
  240.8 1.2 fusion.9
  242.0 0.9 copy-done.4
  242.9 2.9 fusion.2
  245.9 2.5 reshape_transpose_reshape.8
  248.4 5.7 %all-to-all-start.1 = ((bf16[64,4,1792]{2,1,0:T(4,128)(2,1)}), bf16[64,4,1792]{2,1,0:T(4,128)(2,1)S(1)}, u32[]{:S(2)}, u32[]{:S(2)}) async-start(bf16[64,4,1792]{2,1,0:T(4,128)(2,1)} %reshape_transpose_reshape.8), calls=%async_computation.2 | async-start | bytes 1835008 | tf_op jit(solution)/shard_map/all_to_all | solution.py:79
  254.2 32.9 %reduce-scatter.5.cloned.1.call-done = bf16[1,256,1792]{2,1,0:T(8,128)(2,1)} async-done(((bf16[1,256,7168]{2,1,0:T(8,128)(2,1)}), bf16[1,256,1792]{2,1,0:T(8,128)(2,1)}) %reduce-scatter.5.cloned.1.call-update) | async-done | bytes 917520 | tf_op jit(solution)/shard_map/reduce_scatter | solution.py:86
  287.1 2.5 reshape_transpose_reshape.9
  289.6 10.7 %all-to-all-start.4 = ((bf16[64,4,1792]{2,1,0:T(4,128)(2,1)}), bf16[64,4,1792]{2,1,0:T(4,128)(2,1)S(1)}, u32[]{:S(2)}, u32[]{:S(2)}) async-start(bf16[64,4,1792]{2,1,0:T(4,128)(2,1)} %reshape_transpose_reshape.9), calls=%async_computation.6 | async-start | bytes 1835008 | tf_op jit(solution)/shard_map/all_to_all | solution.py:89
  300.6 0.9 gather_fusion.1
  301.5 24.5 %all-to-all-done.4 = bf16[64,4,1792]{2,1,0:T(4,128)(2,1)S(1)} async-done(((bf16[64,4,1792]{2,1,0:T(4,128)(2,1)}), bf16[64,4,1792]{2,1,0:T(4,128)(2,1)S(1)}, u32[]{:S(2)}, u32[]{:S(2)}) %all-to-all-start.4) | async-done | bytes 917536 | tf_op jit(solution)/shard_map/all_to_all | solution.py:89
  326.2 0.9 gather_fusion.3
  327.2 1.4 fusion.13
  (35 shorter events, 3.1 us)
Async XLA Ops:
  8.7 30.0 %all-to-all-start.2 = ((bf16[4,16,1792]{2,1,0:T(8,128)(2,1)}), bf16[4,16,1792]{2,1,0:T(8,128)(2,1)S(1)}, u32[]{:S(2)}, u32[]{:S(2)}) async-start(bf16[4,16,1792]{2,1,0:T(8,128)(2,1)} %stack.2), calls=%async_computation.3 | async-start | bytes 458752 | tf_op jit(solution)/shard_map/all_to_all | solution.py:52
  38.7 100.4 %all-to-all-start = ((bf16[64,4,7168]{2,1,0:T(4,128)(2,1)}), bf16[64,4,7168]{2,1,0:T(4,128)(2,1)}, u32[]{:S(2)}, u32[]{:S(2)}) async-start(bf16[64,4,7168]{2,1,0:T(4,128)(2,1)} %reshape.116), calls=%async_computation | async-start | bytes 7340032 | tf_op jit(solution)/shard_map/all_to_all | solution.py:56
  139.1 90.6 %all-to-all-start.3 = ((bf16[64,4,7168]{2,1,0:T(4,128)(2,1)}), bf16[64,4,7168]{2,1,0:T(4,128)(2,1)}, u32[]{:S(2)}, u32[]{:S(2)}) async-start(bf16[64,4,7168]{2,1,0:T(4,128)(2,1)} %reshape.124), calls=%async_computation.4 | async-start | bytes 7340032 | tf_op jit(solution)/shard_map/all_to_all | solution.py:57
  145.0 100.9 %reduce-scatter.3.cloned.1.call-start = ((), (), s32[]{:S(2)}) async-start(), calls=%async_computation.7 | async-start | bytes 4587520 | tf_op jit(solution)/shard_map/reduce_scatter | solution.py:75
  151.9 4.4 %copy-start = (bf16[256,7168]{1,0:T(8,128)(2,1)S(1)}, bf16[256,7168]{1,0:T(8,128)(2,1)}, u32[]{:S(2)}) copy-start(bf16[256,7168]{1,0:T(8,128)(2,1)} %reshape.117) | copy-start | bytes 11010052
  151.9 5.3 %copy-start.3 = (bf16[1,7168,256]{2,1,0:T(8,128)(2,1)S(1)}, bf16[1,7168,256]{2,1,0:T(8,128)(2,1)}, u32[]{:S(2)}) copy-start(bf16[1,7168,256]{2,1,0:T(8,128)(2,1)} %param.11) | copy-start | bytes 11010052
  157.2 2.0 copy-start.1
  162.3 124.7 %reduce-scatter.5.cloned.1.call-start = ((), (), s32[]{:S(2)}) async-start(), calls=%async_computation.8 | async-start | bytes 4587520 | tf_op jit(solution)/shard_map/reduce_scatter | solution.py:86
  236.4 4.4 %copy-start.2 = (bf16[1,7168,256]{2,1,0:T(8,128)(2,1)S(1)}, bf16[1,7168,256]{2,1,0:T(8,128)(2,1)}, u32[]{:S(2)}) copy-start(bf16[1,7168,256]{2,1,0:T(8,128)(2,1)} %param.10) | copy-start | bytes 11010052
  240.8 2.0 copy-start.4
  245.8 54.5 %copy-start.5 = (f32[16,8]{0,1:T(8,128)S(1)}, f32[16,8]{0,1:T(8,128)}, u32[]{:S(2)}) copy-start(f32[16,8]{0,1:T(8,128)} %param.9) | copy-start | bytes 1540
  248.4 41.2 %all-to-all-start.1 = ((bf16[64,4,1792]{2,1,0:T(4,128)(2,1)}), bf16[64,4,1792]{2,1,0:T(4,128)(2,1)S(1)}, u32[]{:S(2)}, u32[]{:S(2)}) async-start(bf16[64,4,1792]{2,1,0:T(4,128)(2,1)} %reshape_transpose_reshape.8), calls=%async_computation.2 | async-start | bytes 1835008 | tf_op jit(solution)/shard_map/all_to_all | solution.py:79
  289.6 36.4 %all-to-all-start.4 = ((bf16[64,4,1792]{2,1,0:T(4,128)(2,1)}), bf16[64,4,1792]{2,1,0:T(4,128)(2,1)S(1)}, u32[]{:S(2)}, u32[]{:S(2)}) async-start(bf16[64,4,1792]{2,1,0:T(4,128)(2,1)} %reshape_transpose_reshape.9), calls=%async_computation.6 | async-start | bytes 1835008 | tf_op jit(solution)/shard_map/all_to_all | solution.py:89
Sparse Core Ops, SparseCore 0:
  162.5 45.5 reduce-scatter.2
  245.9 41.0 reduce-scatter.4
